TPU v7x, 256 devices: a whole 4x4x8 slice. The times are simulated.
256 devices in a mesh: ctx: 8 (over x, y_hi), mp: 32 (over y_lo, z, core).
Axes of the slice: x: 4, y: 4 (y_hi: 2, y_lo: 2; y = y_hi * 2 + y_lo), z: 8, core: 2. Of those that a mesh axis runs over, the one named last changes fastest.
Arguments:
- hidden_states: bfloat16 [24576, 8192], P('ctx', 'mp'), may hold values from -8 to 8
- route_slot: int32 [4608], P('ctx'), may hold values from 0 to 3071, as said below
- route_live: int32 [4608], P('ctx'), may hold values from 0 to 1, as said below
- router_weight: bfloat16 [8192], replicated, may hold values from -0.0625 to 0.0625
- query_weight: bfloat16 [8192, 8192], P(None, 'mp')
- keyval_weight: bfloat16 [8192, 2048], P(None, 'mp')
- output_weight: bfloat16 [8192, 8192], P('mp'), may hold values from -0.75 to 0.75
Outputs:
- mixed_states: bfloat16 [24576, 8192], P('ctx', 'mp')
Inputs may be any that keep to these rules, and one draw needn't show every extreme that they name: `route_slot`: within each owner's 576 slots the live slots come first and hold distinct ascending offsets below 3072; dead slots hold 0. The last token of every owner is routed. `route_live`: each owner has from 192 to 576 live slots, all at its first slots; together they are exactly 3072; some owner has all 576 live.
All inputs are finite; a program needn't handle non-finite values.
Results may differ from a plain program's by a relative error of at most 0.03.
Values may be sent and summed in bfloat16 or wider, within the bound.
No kernel may reach another device: no remote copies, remote signals or barrier semaphores. Data moves between devices by JAX's collectives and lax.ppermute only.
A program may use at most 128 MiB of HBM per device.

v0:
```python
import jax
import jax.numpy as jnp
from jax import lax
from jax.sharding import PartitionSpec as P

GROUP = 8
HQ_DEV = 2
far_position = 1073741824


def partner_2(value, axis, apart):
    return lax.ppermute(value, axis, [(i, i ^ 1 << apart) for i in range(lax.axis_size(axis))])


def attend_block(state_tuple, queries, query_pos, keyval_rows, key_pos):
    running_max, running_sum, weighted = state_tuple
    width = queries.shape[1]
    key_part = keyval_rows[:, :width]
    value_part = keyval_rows[:, width:]
    scores = lax.dot_general(
        queries, key_part, (((1,), (1,)), ((), ())), preferred_element_type=jnp.float32
    ) * width ** (-0.5)
    allowed = key_pos[None, :] <= query_pos[:, None]
    masked = jnp.where(allowed, scores, -1e30)
    new_max = jnp.maximum(running_max, jnp.max(masked, axis=1))
    weights = jnp.where(allowed, jnp.exp(masked - new_max[:, None]), 0.0)
    shrink = jnp.exp(running_max - new_max)
    running_sum = running_sum * shrink + jnp.sum(weights, axis=1)
    weighted = weighted * shrink[:, None] + jnp.dot(
        weights.astype(jnp.bfloat16), value_part, preferred_element_type=jnp.float32
    )
    return (new_max, running_sum, weighted)


def routed_update(
    routed_rows, positions, router_weight, query_weight, keyval_weight, output_weight
):
    row_total = routed_rows.shape[0]
    local_width = query_weight.shape[1]
    head_width = keyval_weight.shape[1] * GROUP // (2 * HQ_DEV)
    head_count = local_width // head_width
    fragment = lax.all_gather(routed_rows, "mp", axis=1, tiled=True)
    keyval_rows = keyval_weight
    query_acc = jnp.dot(fragment, query_weight, preferred_element_type=jnp.float32)
    keyval_acc = jnp.dot(fragment, keyval_rows, preferred_element_type=jnp.float32)
    logit_acc = jnp.dot(fragment, router_weight, preferred_element_type=jnp.float32)
    query_acc, keyval_acc, logit_acc = (query_acc, keyval_acc, logit_acc)
    queries = query_acc.astype(jnp.bfloat16)
    stacked_queries = (
        queries.reshape(row_total, head_count, head_width)
        .transpose(1, 0, 2)
        .reshape(head_count * row_total, head_width)
    )
    stacked_pos = jnp.tile(positions, head_count)
    own_keyval = keyval_acc.astype(jnp.bfloat16)
    mp_index = lax.axis_index("mp")
    bit_count = (GROUP // HQ_DEV).bit_length() - 1
    for bit_number in range(bit_count):
        partner = partner_2(own_keyval, "mp", bit_number)
        upper_side = mp_index >> bit_number & 1 == 1
        own_keyval = jnp.where(
            upper_side,
            jnp.concatenate([partner, own_keyval], axis=1),
            jnp.concatenate([own_keyval, partner], axis=1),
        )
    stacked_rows = head_count * row_total
    start_state = (
        jnp.full((stacked_rows,), -1e30, jnp.float32),
        jnp.zeros((stacked_rows,), jnp.float32),
        jnp.zeros((stacked_rows, head_width), jnp.float32),
    )
    state_tuple = start_state
    keyval_rows = lax.all_gather(own_keyval, "ctx", axis=0, tiled=True)
    key_pos = lax.all_gather(positions, "ctx", axis=0, tiled=True)
    amount = keyval_rows.shape[0]
    blocks = amount // 512

    def step_block(inner, item):
        return (attend_block(inner, stacked_queries, stacked_pos, item[0], item[1]), None)

    stacked = (keyval_rows.reshape(blocks, 512, keyval_rows.shape[1]), key_pos.reshape(blocks, 512))
    state_tuple, unused = lax.scan(step_block, state_tuple, stacked)
    running_max, running_sum, weighted = state_tuple
    stacked_attended = (weighted / running_sum[:, None]).astype(jnp.bfloat16)
    attended = (
        stacked_attended.reshape(head_count, row_total, head_width)
        .transpose(1, 0, 2)
        .reshape(row_total, local_width)
    )
    gate_value = jax.nn.sigmoid(logit_acc)
    combined = lax.psum_scatter(
        lax.dot_general(
            output_weight, attended, (((0,), (1,)), ((), ())), preferred_element_type=jnp.float32
        ).astype(jnp.bfloat16),
        "mp",
        scatter_dimension=0,
        tiled=True,
    ).astype(jnp.float32)
    return (gate_value[:, None] * combined.T).astype(jnp.bfloat16)


def local(
    hidden_states, route_slot, route_live, router_weight, query_weight, keyval_weight, output_weight
):
    seq_dev = hidden_states.shape[0]
    ctx_id = lax.axis_index("ctx")
    own_rows = jnp.take(hidden_states, route_slot, axis=0)
    positions = jnp.where(route_live == 1, ctx_id * seq_dev + route_slot, far_position)
    update = routed_update(
        own_rows, positions, router_weight, query_weight, keyval_weight, output_weight
    )
    addition = jnp.where(route_live[:, None] == 1, update.astype(jnp.float32), 0.0)
    widened = hidden_states.astype(jnp.float32).at[route_slot].add(addition)
    return widened.astype(jnp.bfloat16)


def solution(mesh):
    placed = (P("ctx", "mp"), P("ctx"), P("ctx"), P(), P(None, "mp"), P(None, "mp"), P("mp", None))
    return jax.shard_map(
        local, mesh=mesh, in_specs=placed, out_specs=P("ctx", "mp"), check_vma=False
    )
```

profile of v0, /device:TPU:20, one launch (start us, length us, event | category | flops | bytes accessed | tf_op | source)
XLA Modules:
  0.0 374.4 jit_solution(8200890812531677743)
XLA Ops:
  6.5 0.8 compare_and_fusion
  7.3 1.3 dynamic-slice
  9.2 0.8 fusion.25
  10.1 3.8 %gather_fusion = bf16[576,256]{1,0:T(8,128)(2,1)S(1)} fusion(bf16[3072,256]{1,0:T(8,128)(2,1)} %param.9, s32[1024]{0:T(1024)S(1)} %pad_clamp_fusion), kind=kCustom, calls=%fused_computation | custom fusion | bytes 592128 | tf_op jit(solution)/shard_map/jit(_take)/gather | solution.py:107
  13.9 0.9 broadcast_select_fusion
  14.8 96.4 %all-gather.3.cloned.1.call-done = bf16[576,8192]{1,0:T(8,128)(2,1)} async-done(((bf16[576,256]{1,0:T(8,128)(2,1)}), bf16[576,8192]{1,0:T(8,128)(2,1)}) %all-gather.3.cloned.1.call-update) | async-done | bytes 9437200 | tf_op jit(solution)/shard_map/all_gather | solution.py:42
  111.2 6.6 %convolution_convert_fusion.2 = bf16[576,64]{0,1:T(8,128)(2,1)S(1)} fusion(bf16[576,8192]{1,0:T(8,128)(2,1)} %all-gather.3.cloned.1.call-done, bf16[8192,64]{0,1:T(8,128)(2,1)S(1)} %copy-done), kind=kOutput, calls=%fused_computation.27 | convolution fusion | flops 604016640 | bytes 10559488 | tf_op jit(solution)/shard_map/dot_general | solution.py:45
  117.8 0.3 collective-permute-start
  118.1 1.0 collective-permute-done
  119.2 2.2 collective-permute-start.1
  121.4 4.6 %collective-permute-done.1 = bf16[576,128]{0,1:T(8,128)(2,1)S(1)} collective-permute-done((bf16[576,128]{0,1:T(8,128)(2,1)S(1)}, bf16[576,128]{0,1:T(8,128)(2,1)S(1)}, u32[]{:S(2)}, u32[]{:S(2)}) %collective-permute-start.1) | collective-permute-done | bytes 147488 | tf_op jit(solution)/shard_map/ppermute | solution.py:12
  126.1 0.9 copy.13
  127.0 34.8 %all-reduce = s32[4608]{0:T(1024)S(1)} all-reduce(s32[4608]{0:T(1024)S(1)} %get-tuple-element.106), channel_id=1, replica_groups=mesh['ctx'=8,'mp'=32] {'ctx'}, use_global_device_ids=true, to_apply=%add | all-reduce | flops 4608 | bytes 36864
  161.8 7.8 %convolution_convert_fusion.1 = bf16[576,256]{1,0:T(8,128)(2,1)S(1)} fusion(bf16[576,8192]{1,0:T(8,128)(2,1)} %all-gather.3.cloned.1.call-done, bf16[8192,256]{1,0:T(8,128)(2,1)} %param.13), kind=kOutput, calls=%fused_computation.26 | convolution fusion | flops 2416066560 | bytes 13926400 | tf_op jit(solution)/shard_map/dot_general | solution.py:44
  169.7 14.9 %all-gather.5.cloned.1.call-done = bf16[4608,256]{1,0:T(8,128)(2,1)} async-done(((bf16[576,256]{1,0:T(8,128)(2,1)}), bf16[4608,256]{1,0:T(8,128)(2,1)}) %all-gather.5.cloned.1.call-update) | async-done | bytes 2359312 | tf_op jit(solution)/shard_map/all_gather | solution.py:73
  184.6 27.0 %while.15 = (s32[]{:T(128)}, f32[1152]{0:T(1024)S(1)}, f32[1152]{0:T(1024)S(1)}, f32[1152,128]{1,0:T(8,128)S(1)}, s32[9,512]{1,0:T(8,128)S(1)}, /*index=5*/bf16[...) while((s32[]{:T(128)}, f32[1152]{0:T(1024)S(1)}, ...), condition=%wide.region_3.4_spmd.clone, body=%wide.region_0.3_spmd.clone.sunk | while | flops 309515904 | bytes 9467265 | solution.py:82
  184.7 0.1 le.67
  184.7 1.0 dynamic-slice_bitcast_fusion.2
  185.7 0.5 fusion.44
  186.3 0.5 fusion.45
  186.8 0.8 convolution_add_fusion.2
  187.7 0.1 le.67
  187.7 1.0 dynamic-slice_bitcast_fusion.2
  188.7 0.5 fusion.44
  189.3 0.5 fusion.45
  189.8 0.8 convolution_add_fusion.2
  190.7 0.1 le.67
  190.8 1.0 dynamic-slice_bitcast_fusion.2
  191.7 0.5 fusion.44
  192.3 0.5 fusion.45
  192.8 0.8 convolution_add_fusion.2
  193.8 1.0 dynamic-slice_bitcast_fusion.2
  194.7 0.5 fusion.44
  195.3 0.5 fusion.45
  195.8 0.8 convolution_add_fusion.2
  196.8 1.0 dynamic-slice_bitcast_fusion.2
  197.7 0.5 fusion.44
  198.3 0.5 fusion.45
  198.8 0.8 convolution_add_fusion.2
  199.8 1.0 dynamic-slice_bitcast_fusion.2
  200.8 0.5 fusion.44
  201.3 0.5 fusion.45
  201.8 0.8 convolution_add_fusion.2
  202.8 1.0 dynamic-slice_bitcast_fusion.2
  203.8 0.5 fusion.44
  204.3 0.5 fusion.45
  204.8 0.8 convolution_add_fusion.2
  205.8 1.0 dynamic-slice_bitcast_fusion.2
  206.8 0.5 fusion.44
  207.3 0.5 fusion.45
  207.8 0.8 convolution_add_fusion.2
  208.8 1.0 dynamic-slice_bitcast_fusion.2
  209.8 0.5 fusion.44
  210.3 0.5 fusion.45
  210.8 0.8 convolution_add_fusion.2
  211.7 0.2 divide_convert_fusion
  211.9 0.3 copy.15
  212.2 7.3 %fusion.15 = bf16[8192,576]{0,1:T(8,128)(2,1)} fusion(bf16[256,8192]{1,0:T(8,128)(2,1)} %param.15, bf16[72,8,2,128]{3,2,1,0:T(2,128)(2,1)S(1)} %bitcast.36), kind=kOutput, calls=%fused_computation.25 | convolution fusion | flops 2420637696 | bytes 13926400 | tf_op jit(solution)/shard_map/dot_general | solution.py:92
  219.5 1.4 copy-done.1
  220.9 1.9 convert_element_type.35
  222.9 6.2 %convolution_reduce_fusion = f32[576]{0:T(1024)S(1)} fusion(bf16[576,8192]{1,0:T(8,128)(2,1)} %all-gather.3.cloned.1.call-done, bf16[8192,1]{0,1:T(2,128)(2,1)S(1)} %reshape.60), kind=kOutput, calls=%fused_computation.28 | convolution fusion | flops 9437184 | bytes 9455872 | tf_op jit(solution)/shard_map/dot_general | solution.py:46
  229.1 124.3 %reduce-scatter.2.cloned.1.call-done = bf16[256,576]{0,1:T(8,128)(2,1)} async-done(((bf16[8192,576]{0,1:T(8,128)(2,1)}), bf16[256,576]{0,1:T(8,128)(2,1)}) %reduce-scatter.2.cloned.1.call-update) | async-done | bytes 294928 | tf_op jit(solution)/shard_map/reduce_scatter | solution.py:91
  353.4 11.3 %scatter_custom_fusion = f32[3072,256]{1,0:T(8,128)} fusion(f32[3072,256]{1,0:T(8,128)} %convert_element_type.35, s32[576]{0:T(1024)S(1)} %get-tuple-element.111, bf16[256,576]{0,1:T(8,128)(2,1)} %reduce-scatter.2.cloned.1.call-done, f32[]{:T(128)} %constant.33.clone.1, f32[576]{0:T(1024)S(1)} %add_divide_fusion, pred[576]{0:T(1024)(128)(4,1)S(1)} %get-tuple-element.108), kind=kCustom, calls=%fused_computation.29 | custom fusion | flops 884736 | bytes 3446272 | tf_op jit(solution)/shard_map/scatter-add | solution.py:113
  364.7 3.2 convert_element_type.44
  (74 shorter events, 1.2 us)
Async XLA Ops:
  6.5 104.7 %copy-start = (bf16[8192,64]{0,1:T(8,128)(2,1)S(1)}, bf16[8192,64]{0,1:T(8,128)(2,1)}, u32[]{:S(2)}) copy-start(bf16[8192,64]{0,1:T(8,128)(2,1)} %param.14) | copy-start | bytes 3145732
  6.5 104.7 %all-gather.3.cloned.1.call-start = ((), (), s32[]{:S(2)}) async-start(), calls=%async_computation.1 | async-start | bytes 9732096 | tf_op jit(solution)/shard_map/all_gather | solution.py:42
  14.7 169.9 %all-gather.5.cloned.1.call-start = ((), (), s32[]{:S(2)}) async-start(), calls=%async_computation.2 | async-start | bytes 2654208 | tf_op jit(solution)/shard_map/all_gather | solution.py:73
  117.8 1.4 collective-permute-start
  119.2 6.8 %collective-permute-start.1 = (bf16[576,128]{0,1:T(8,128)(2,1)S(1)}, bf16[576,128]{0,1:T(8,128)(2,1)S(1)}, u32[]{:S(2)}, u32[]{:S(2)}) collective-permute-start(bf16[576,128]{0,1:T(8,128)(2,1)S(1)} %maximum_select_fusion.1), channel_id=1, source_target_pairs={{0,2},{1,3},{2,0},{3,1},{4,6},{5,7},{6,4},{7,5},{8,10},{9,11},{10,... | collective-permute-start | bytes 442376 | tf_op jit(solution)/shard_map/ppermute | solution.py:12
  127.0 226.5 %reduce-scatter.2.cloned.1.call-start = ((), (), s32[]{:S(2)}) async-start(), calls=%async_computation.3 | async-start | bytes 9732096 | tf_op jit(solution)/shard_map/reduce_scatter | solution.py:91
  219.5 1.4 copy-start.1
  220.9 1.9 copy-start.2
Sparse Core Ops, SparseCore 0:
  14.9 96.2 all-gather.2
  127.1 57.5 all-gather.4
  219.7 133.7 reduce-scatter.1
where the time goes:
time: 375 us; the launch traced here: 374 us
  waiting for transfers between devices  241 us (64%)
  matrix products  40.1 us (11%)
  blocking collectives  34.8 us (9%)
  other arithmetic  23.8 us (6%)
  local copies, waits for them, and re-layouts  17.3 us (5%)
  between operations  13.9 us (4%)
    reduce_scatter x1, waiting for transfers between devices, routed_update(): lax.psum_scatter(lax.dot_general(output_weight, attended, (((0,), (1,)),...  124 us
    all_gather x1, waiting for transfers between devices, routed_update(): fragment = lax.all_gather(routed_rows, 'mp', axis=1, tiled=True)  96.4 us
    unnamed x1, blocking collectives  34.8 us
    all_gather x1, waiting for transfers between devices, routed_update(): keyval_rows = lax.all_gather(own_keyval, 'ctx', axis=0, tiled=True)  14.9 us
    scatter-add x1, other arithmetic, local(): widened = hidden_states.astype(jnp.float32).at[route_slot].add(addition)  11.3 us
    squeeze x9, local copies, waits for them, and re-layouts, routed_update(): state_tuple, unused = lax.scan(step_block, state_tuple, stacked)  8.71 us
    dot_general x1, matrix products, routed_update(): jnp.dot(fragment, query_weight, preferred_element_type=jnp.float32)  7.76 us
    dot_general x9, matrix products, attend_block(): jnp.dot(weights.astype(jnp.bfloat16), value_part, preferred_element_type=...  7.55 us
  transfers between devices with their start and end apart: 5, of which 5 were waited for; matrix products, arithmetic and copies ran while one was open for 4% of the time, Pallas kernels for 0%

commit v1 on v0

--- a/solution.py
+++ b/solution.py
@@ -70,7 +70,9 @@
         jnp.zeros((stacked_rows, head_width), jnp.float32),
     )
     state_tuple = start_state
-    keyval_rows = lax.all_gather(own_keyval, "ctx", axis=0, tiled=True)
+    keyval_rows = jnp.concatenate(
+        lax.all_to_all(jnp.stack([own_keyval] * lax.axis_size("ctx")), "ctx", 0, 0), axis=0
+    )
     key_pos = lax.all_gather(positions, "ctx", axis=0, tiled=True)
     amount = keyval_rows.shape[0]
     blocks = amount // 512

time: 375 us -> 401 us (1.069)
  blocking collectives: 34.8 us -> 57.5 us
  waiting for transfers between devices: 241 us -> 223 us
  matrix products: 40.1 us -> 49.7 us
  starting transfers between devices: 2.59 us -> 9.72 us
    unnamed x1, blocking collectives: 34.8 us -> 57.5 us
    all_gather x1 -> x0, waiting for transfers between devices: 14.9 us -> none  [routed_update(): keyval_rows = lax.all_gather(own_keyval, 'ctx', axis=0, tiled=True)]
    dot_general x9, matrix products: 4.71 us -> 13.9 us  [attend_block(): lax.dot_general(queries, key_part, (((1,), (1,)), ((), ())), preferred_el...]
    squeeze x9, local copies, waits for them, and re-layouts: 8.71 us -> 0.16 us  [routed_update(): state_tuple, unused = lax.scan(step_block, state_tuple, stacked)]
    while x9 -> x45, local copies, waits for them, and re-layouts: 0.02 us -> 7.27 us
    all_to_all x0 -> x1, starting transfers between devices: none -> 7.21 us  [routed_update(): lax.all_to_all(jnp.stack([own_keyval] * lax.axis_size('ctx')), 'ctx', 0, 0)]
  transfers between devices with their start and end apart: 5 -> 5, of which waited for: 5 -> 4; matrix products, arithmetic and copies ran while one was open for 4% -> 5% of each run, Pallas kernels for 0% -> 0%
where the time goes in v1:
time: 401 us; the launch traced here: 400 us
  waiting for transfers between devices  223 us (56%)
  blocking collectives  57.5 us (14%)
  matrix products  49.7 us (12%)
  other arithmetic  24.9 us (6%)
  local copies, waits for them, and re-layouts  20.2 us (5%)
  between operations  14.1 us (4%)
  starting transfers between devices  9.72 us (2%)
    reduce_scatter x1, waiting for transfers between devices, routed_update(): lax.psum_scatter(lax.dot_general(output_weight, attended, (((0,), (1,)),...  121 us
    all_gather x1, waiting for transfers between devices, routed_update(): fragment = lax.all_gather(routed_rows, 'mp', axis=1, tiled=True)  96.4 us
    unnamed x1, blocking collectives  57.5 us
    dot_general x9, matrix products, attend_block(): lax.dot_general(queries, key_part, (((1,), (1,)), ((), ())), preferred_el...  13.9 us
    scatter-add x1, other arithmetic, local(): widened = hidden_states.astype(jnp.float32).at[route_slot].add(addition)  11.3 us
    dot_general x1, matrix products, routed_update(): jnp.dot(fragment, query_weight, preferred_element_type=jnp.float32)  8.18 us
  transfers between devices with their start and end apart: 5, of which 4 were waited for; matrix products, arithmetic and copies ran while one was open for 5% of the time, Pallas kernels for 0%

profile of v1, /device:TPU:20, one launch (start us, length us, event | category | flops | bytes accessed | tf_op | source)
XLA Modules:
  0.0 399.6 jit_solution(13527398318436526223)
XLA Ops:
  6.5 0.8 compare_and_fusion
  7.3 1.3 dynamic-slice
  9.2 0.8 fusion.25
  10.1 3.8 gather_fusion
  13.9 0.9 broadcast_select_fusion
  14.8 96.4 %all-gather.2.cloned.1.call-done = bf16[576,8192]{1,0:T(8,128)(2,1)} async-done(((bf16[576,256]{1,0:T(8,128)(2,1)}), bf16[576,8192]{1,0:T(8,128)(2,1)}) %all-gather.2.cloned.1.call-update) | async-done | bytes 9437200 | tf_op jit(solution)/shard_map/all_gather | solution.py:42
  111.2 6.6 %convolution_convert_fusion.2 = bf16[576,64]{0,1:T(8,128)(2,1)S(1)} fusion(bf16[576,8192]{1,0:T(8,128)(2,1)} %all-gather.2.cloned.1.call-done, bf16[8192,64]{0,1:T(8,128)(2,1)S(1)} %copy-done), kind=kOutput, calls=%fused_computation.27 | convolution fusion | flops 604016640 | bytes 10559488 | tf_op jit(solution)/shard_map/dot_general | solution.py:45
  117.8 0.3 collective-permute-start
  118.1 1.0 collective-permute-done
  119.2 2.2 collective-permute-start.1
  121.4 4.6 %collective-permute-done.1 = bf16[576,128]{0,1:T(8,128)(2,1)S(1)} collective-permute-done((bf16[576,128]{0,1:T(8,128)(2,1)S(1)}, bf16[576,128]{0,1:T(8,128)(2,1)S(1)}, u32[]{:S(2)}, u32[]{:S(2)}) %collective-permute-start.1) | collective-permute-done | bytes 147488 | tf_op jit(solution)/shard_map/ppermute | solution.py:12
  126.1 0.2 copy.10
  126.2 1.6 stack.2
  127.8 7.2 %all-to-all-start = ((bf16[8,576,256]{2,1,0:T(8,128)(2,1)}), bf16[8,576,256]{2,1,0:T(8,128)(2,1)S(1)}, u32[]{:S(2)}, u32[]{:S(2)}) async-start(bf16[8,576,256]{2,1,0:T(8,128)(2,1)} %stack.2), calls=%async_computation | async-start | bytes 4718592 | tf_op jit(solution)/shard_map/all_to_all | solution.py:74
  135.0 57.5 %all-reduce = s32[4608]{0:T(1024)S(1)} all-reduce(s32[4608]{0:T(1024)S(1)} %get-tuple-element.98), channel_id=1, replica_groups=mesh['ctx'=8,'mp'=32] {'ctx'}, use_global_device_ids=true, to_apply=%add | all-reduce | flops 4608 | bytes 36864
  192.5 8.2 %convolution_convert_fusion.1 = bf16[576,256]{1,0:T(8,128)(2,1)} fusion(bf16[576,8192]{1,0:T(8,128)(2,1)} %all-gather.2.cloned.1.call-done, bf16[8192,256]{1,0:T(8,128)(2,1)} %param.13), kind=kOutput, calls=%fused_computation.26 | convolution fusion | flops 2416066560 | bytes 13926400 | tf_op jit(solution)/shard_map/dot_general | solution.py:44
  200.6 1.7 reshape.42
  202.4 1.7 copy.11
  204.1 34.9 %while.15 = (s32[]{:T(128)}, f32[1152]{0:T(1024)S(1)}, f32[1152]{0:T(1024)S(1)}, f32[1152,128]{1,0:T(8,128)}, s32[9,512]{1,0:T(8,128)S(1)}, /*index=5*/bf16[9,51...) while((s32[]{:T(128)}, f32[1152]{0:T(1024)S(1)}, ...), condition=%wide.region_3.4_spmd.clone, body=%wide.region_0.3_spmd.clone.sunk | while | flops 309515904 | bytes 14185913 | solution.py:84
  204.2 1.6 fusion.44
  205.8 0.5 fusion.45
  206.3 0.8 convolution_add_fusion.2
  207.2 0.8 copy-done.3
  208.1 1.5 fusion.44
  209.7 0.5 fusion.45
  210.2 0.8 convolution_add_fusion.2
  211.1 0.8 copy-done.3
  212.0 1.5 fusion.44
  213.6 0.5 fusion.45
  214.1 0.8 convolution_add_fusion.2
  215.0 0.8 copy-done.3
  215.9 1.5 fusion.44
  217.4 0.5 fusion.45
  218.0 0.8 convolution_add_fusion.2
  218.8 0.8 copy-done.3
  219.8 1.5 fusion.44
  221.3 0.5 fusion.45
  221.8 0.8 convolution_add_fusion.2
  222.7 0.8 copy-done.3
  223.6 1.6 fusion.44
  225.2 0.5 fusion.45
  225.7 0.8 convolution_add_fusion.2
  226.6 0.8 copy-done.3
  227.5 1.6 fusion.44
  229.1 0.5 fusion.45
  229.6 0.8 convolution_add_fusion.2
  230.5 0.8 copy-done.3
  231.4 1.6 fusion.44
  233.0 0.5 fusion.45
  233.5 0.8 convolution_add_fusion.2
  234.4 0.8 copy-done.3
  235.3 1.6 fusion.44
  236.8 0.5 fusion.45
  237.4 0.8 convolution_add_fusion.2
  238.2 0.8 copy-done.3
  239.0 1.3 divide_convert_fusion
  240.3 0.3 copy.12
  240.6 7.3 %fusion.15 = bf16[8192,576]{0,1:T(8,128)(2,1)} fusion(bf16[256,8192]{1,0:T(8,128)(2,1)} %param.15, bf16[72,8,2,128]{3,2,1,0:T(2,128)(2,1)S(1)} %bitcast.37), kind=kOutput, calls=%fused_computation.25 | convolution fusion | flops 2420637696 | bytes 13926400 | tf_op jit(solution)/shard_map/dot_general | solution.py:94
  247.9 1.4 copy-done.1
  249.3 1.9 convert_element_type.35
  251.3 6.2 %convolution_reduce_fusion = f32[576]{0:T(1024)S(1)} fusion(bf16[576,8192]{1,0:T(8,128)(2,1)} %all-gather.2.cloned.1.call-done, bf16[8192,1]{0,1:T(2,128)(2,1)S(1)} %reshape.69), kind=kOutput, calls=%fused_computation.28 | convolution fusion | flops 9437184 | bytes 9455872 | tf_op jit(solution)/shard_map/dot_general | solution.py:46
  257.5 120.8 %reduce-scatter.2.cloned.1.call-done = bf16[256,576]{0,1:T(8,128)(2,1)} async-done(((bf16[8192,576]{0,1:T(8,128)(2,1)}), bf16[256,576]{0,1:T(8,128)(2,1)}) %reduce-scatter.2.cloned.1.call-update) | async-done | bytes 294928 | tf_op jit(solution)/shard_map/reduce_scatter | solution.py:93
  378.3 11.3 %scatter_custom_fusion = f32[3072,256]{1,0:T(8,128)} fusion(f32[3072,256]{1,0:T(8,128)} %convert_element_type.35, s32[576]{0:T(1024)S(1)} %get-tuple-element.103, bf16[256,576]{0,1:T(8,128)(2,1)} %reduce-scatter.2.cloned.1.call-done, f32[]{:T(128)} %constant.33.clone.1, f32[576]{0:T(1024)S(1)} %add_divide_fusion, pred[576]{0:T(1024)(128)(4,1)S(1)} %get-tuple-element.100), kind=kCustom, calls=%fused_computation.29 | custom fusion | flops 884736 | bytes 3446272 | tf_op jit(solution)/shard_map/scatter-add | solution.py:115
  389.5 3.2 convert_element_type.44
  (110 shorter events, 1.4 us)
Async XLA Ops:
  6.5 104.7 %copy-start = (bf16[8192,64]{0,1:T(8,128)(2,1)S(1)}, bf16[8192,64]{0,1:T(8,128)(2,1)}, u32[]{:S(2)}) copy-start(bf16[8192,64]{0,1:T(8,128)(2,1)} %param.14) | copy-start | bytes 3145732
  6.5 104.7 %all-gather.2.cloned.1.call-start = ((), (), s32[]{:S(2)}) async-start(), calls=%async_computation.2 | async-start | bytes 9732096 | tf_op jit(solution)/shard_map/all_gather | solution.py:42
  117.8 1.4 collective-permute-start
  119.2 6.8 %collective-permute-start.1 = (bf16[576,128]{0,1:T(8,128)(2,1)S(1)}, bf16[576,128]{0,1:T(8,128)(2,1)S(1)}, u32[]{:S(2)}, u32[]{:S(2)}) collective-permute-start(bf16[576,128]{0,1:T(8,128)(2,1)S(1)} %maximum_select_fusion.1), channel_id=1, source_target_pairs={{0,2},{1,3},{2,0},{3,1},{4,6},{5,7},{6,4},{7,5},{8,10},{9,11},{10,... | collective-permute-start | bytes 442376 | tf_op jit(solution)/shard_map/ppermute | solution.py:12
  127.8 76.3 %all-to-all-start = ((bf16[8,576,256]{2,1,0:T(8,128)(2,1)}), bf16[8,576,256]{2,1,0:T(8,128)(2,1)S(1)}, u32[]{:S(2)}, u32[]{:S(2)}) async-start(bf16[8,576,256]{2,1,0:T(8,128)(2,1)} %stack.2), calls=%async_computation | async-start | bytes 4718592 | tf_op jit(solution)/shard_map/all_to_all | solution.py:74
  135.0 243.3 %reduce-scatter.2.cloned.1.call-start = ((), (), s32[]{:S(2)}) async-start(), calls=%async_computation.3 | async-start | bytes 9732096 | tf_op jit(solution)/shard_map/reduce_scatter | solution.py:93
  204.2 2.1 copy-start.2
  207.2 0.8 copy-start.3
  208.1 2.1 copy-start.2
  211.1 0.8 copy-start.3
  212.0 2.1 copy-start.2
  214.9 0.8 copy-start.3
  215.9 2.1 copy-start.2
  218.8 0.8 copy-start.3
  219.7 2.1 copy-start.2
  222.7 0.8 copy-start.3
  223.6 2.1 copy-start.2
  226.6 0.8 copy-start.3
  227.5 2.1 copy-start.2
  230.5 0.8 copy-start.3
  231.4 2.1 copy-start.2
  234.3 0.8 copy-start.3
  235.3 2.1 copy-start.2
  238.2 0.8 copy-start.3
  247.9 1.4 copy-start.1
  249.3 1.9 copy-start.4
Sparse Core Ops, SparseCore 0:
  14.9 96.2 all-gather.1
  248.0 130.2 reduce-scatter.1
